TPU v7x, 256 devices: a whole 4x4x8 slice. The times are simulated.
256 devices in a mesh: req: 2 (over core), blk: 128 (over z, x, y).
Axes of the slice: x: 4, y: 4, z: 8, core: 2. Of those that a mesh axis runs over, the one named last changes fastest.
Arguments:
- query: bfloat16 [2, 8192, 2048], P('req', 'blk'), may hold values from -64 to 64
- rotated_key_value: bfloat16 [2, 2, 8192, 512], P('req', None, 'blk'), may hold values from -64 to 64
- lengths: int32 [2], P('req'), may hold values from 6144 to 8192, as said below
- block_map: int32 [256], replicated, may hold values from 0 to 255, as said below
- segment_head: int32 [4], replicated, may hold values from 0 to 3, each once
Outputs:
- attended: bfloat16 [2, 8192, 2048], P('req', 'blk')
- cache: bfloat16 [2, 2, 128, 256, 128], P('req', None, 'blk')
Inputs may be any that keep to these rules, and one draw needn't show every extreme that they name: `lengths`: one of the two prompts has exactly 8192 tokens. `block_map`: each prompt block appears once; storage blocks 2d and 2d+1 hold blocks b and 255 - b for some b < 128.
All inputs are finite; a program needn't handle non-finite values.
Results may differ from a plain program's by a relative error of at most 0.007.
Values may be sent and summed in bfloat16 or wider, within the bound.
No kernel may reach another device: no remote copies, remote signals or barrier semaphores. Data moves between devices by JAX's collectives and lax.ppermute only.
A program may use at most 128 MiB of HBM per device.

v0:
```python
import jax
import jax.numpy as jnp
from jax import lax
from jax.sharding import PartitionSpec as P

QUERY_HEADS = 16
KEY_VALUE_HEADS = 4
HEAD_DIMENSION = 128
WINDOW = 4096


def body(query, rotated_key_value, lengths, block_map, segment_head):
    token_index = query.shape[1]
    half_width = token_index // 2
    query_groups = QUERY_HEADS // KEY_VALUE_HEADS
    token_count = lax.axis_size("blk")
    place = lax.axis_index("blk")
    segment_list = token_count // KEY_VALUE_HEADS
    group_repeats = half_width // segment_list
    prompt_blocks = 2 * token_count
    length = lengths[0]
    scale = HEAD_DIMENSION ** (-0.5)
    my_blocks = lax.dynamic_slice_in_dim(block_map, 2 * place, 2)
    qpos = (
        my_blocks[:, None] * half_width + jnp.arange(half_width, dtype=jnp.int32)[None, :]
    ).reshape(token_index)
    query_rows = query[0].reshape(token_index, KEY_VALUE_HEADS, query_groups, HEAD_DIMENSION)
    slot_seg = place % segment_list
    segment_piece = lax.all_gather(rotated_key_value, "blk", axis=2, tiled=True)
    upper_limit = jnp.full((KEY_VALUE_HEADS, query_groups, token_index), -1e30, jnp.float32)
    held = jnp.zeros((2, prompt_blocks, group_repeats, HEAD_DIMENSION), jnp.bfloat16)
    row_indices = segment_piece.shape[2]
    nblock = row_indices // half_width
    owned = jnp.take(block_map, jnp.arange(nblock, dtype=jnp.int32))
    kpos = (owned[:, None] * half_width + jnp.arange(half_width, dtype=jnp.int32)[None, :]).reshape(
        row_indices
    )
    key_rows = segment_piece[0, 0].reshape(row_indices, KEY_VALUE_HEADS, HEAD_DIMENSION)
    value_rows = segment_piece[0, 1].reshape(row_indices, KEY_VALUE_HEADS, HEAD_DIMENSION)
    scores = (
        jnp.einsum("qhgd,khd->hgqk", query_rows, key_rows, preferred_element_type=jnp.float32)
        * scale
    )
    allowed = (kpos[None, :] <= qpos[:, None]) & (kpos[None, :] > qpos[:, None] - WINDOW)
    allowed = allowed & ((kpos[None, :] < length) | (kpos[None, :] == qpos[:, None]))
    allowed = allowed[None, None]
    fresh = jnp.maximum(upper_limit, jnp.max(jnp.where(allowed, scores, -1e30), axis=-1))
    prob = jnp.where(allowed, jnp.exp(scores - fresh[..., None]), 0.0)
    total = jnp.sum(prob, axis=-1)
    summed = jnp.einsum(
        "hgqk,khd->hgqd", prob.astype(jnp.bfloat16), value_rows, preferred_element_type=jnp.float32
    )
    final = (fresh, total, summed, held)
    upper_limit, total, summed, held = final
    result = summed / total[..., None]
    result = jnp.where((qpos < length)[None, None, :, None], result, 0.0)
    attended = (
        result.transpose(2, 0, 1, 3)
        .reshape(1, token_index, QUERY_HEADS * HEAD_DIMENSION)
        .astype(jnp.bfloat16)
    )
    launch_lattice = rotated_key_value[0].reshape(
        2, 2, group_repeats, segment_list, KEY_VALUE_HEADS, HEAD_DIMENSION
    )
    launch_lattice = jnp.take(launch_lattice, segment_head, axis=4)
    outgoing = launch_lattice.transpose(0, 4, 3, 1, 2, 5).reshape(
        2, token_count, 2, group_repeats, HEAD_DIMENSION
    )
    arrived = lax.all_to_all(outgoing, "blk", split_axis=1, concat_axis=1, tiled=True)
    arrived = arrived.reshape(2, prompt_blocks, group_repeats, HEAD_DIMENSION)
    held = (
        jnp.zeros((2, prompt_blocks, group_repeats, HEAD_DIMENSION), jnp.bfloat16)
        .at[:, block_map]
        .set(arrived)
    )
    position = (
        jnp.arange(prompt_blocks, dtype=jnp.int32)[:, None] * group_repeats
        + jnp.arange(group_repeats, dtype=jnp.int32)[None, :]
    ) * segment_list + slot_seg
    held = jnp.where((position < length)[None, :, :, None], held, jnp.zeros((), jnp.bfloat16))
    cache = held.reshape(2, prompt_blocks * group_repeats, HEAD_DIMENSION)[None, :, None]
    return (attended, cache)


def solution(mesh):
    return jax.shard_map(
        body,
        mesh=mesh,
        in_specs=(P("req", "blk", None), P("req", None, "blk", None), P("req"), P(), P()),
        out_specs=(P("req", "blk", None), P("req", None, "blk", None, None)),
        check_vma=False,
    )
```

profile of v0, /device:TPU:1, one launch (start us, length us, event | category | flops | bytes accessed | tf_op | source)
XLA Modules:
  0.0 320.5 jit_solution(6120186794051382634)
XLA Ops:
  7.2 0.0 all-gather.2.cloned.1.call-start
  7.2 1.7 copy.26
  8.9 0.0 all-gather.2.cloned.1.call-update
  8.9 0.9 reshape.238
  9.9 0.7 compare_select_fusion.1
  10.6 0.6 gather_fusion.1
  11.1 0.7 compare_and_fusion
  11.8 0.1 fusion.22
  11.9 0.8 copy.35
  12.7 16.5 %all-to-all-start = ((bf16[2,128,2,1,128]{4,2,0,3,1:T(2,128)(2,1)}), bf16[2,128,2,1,128]{4,2,0,3,1:T(2,128)(2,1)S(1)}, u32[]{:S(2)}, u32[]{:S(2)}) async-start(bf16[2,128,2,1,128]{4,2,0,3,1:T(2,128)(2,1)} %copy.35), calls=%async_computation | async-start | bytes 262144 | tf_op jit(solution)/shard_map/all_to_all | solution.py:69
  29.3 2.0 gather_fusion
  31.3 0.1 iota_add_fusion
  31.4 0.1 add.100
  31.5 0.8 dynamic-slice_multiply_fusion
  32.2 0.1 iota_add_fusion.1
  32.3 0.1 add.96
  33.1 0.8 or_and_fusion
  33.9 1.1 reshape_squeeze.13
  35.0 0.7 compare_select_fusion
  35.7 4.6 %all-to-all-done = bf16[2,128,2,1,128]{4,2,0,3,1:T(2,128)(2,1)S(1)} async-done(((bf16[2,128,2,1,128]{4,2,0,3,1:T(2,128)(2,1)}), bf16[2,128,2,1,128]{4,2,0,3,1:T(2,128)(2,1)S(1)}, u32[]{:S(2)}, u32[]{:S(2)}) %all-to-all-start) | async-done | bytes 131104 | tf_op jit(solution)/shard_map/all_to_all | solution.py:69
  40.3 0.1 copy.36
  40.4 0.1 copy.37
  40.5 0.1 broadcast.181
  40.6 7.2 %scatter_fusion = bf16[2,256,128]{2,0,1:T(2,128)(2,1)S(1)} fusion(bf16[2,256,128]{2,0,1:T(2,128)(2,1)S(1)} %broadcast.181, s32[256]{0:T(256)S(1)} %compare_select_fusion, bf16[256,2,128]{2,1,0:T(2,128)(2,1)S(1)} %copy.37), kind=kCustom, calls=%fused_computation.2 | custom fusion | bytes 394240 | tf_op jit(solution)/shard_map/scatter | solution.py:74
  47.8 0.3 fusion.23
  48.1 0.7 copy.38
  48.8 117.2 %all-gather.2.cloned.1.call-done = bf16[1,2,8192,512]{3,1,0,2:T(2,128)(2,1)} async-done(((bf16[1,2,64,512]{3,1,0,2:T(2,128)(2,1)}), bf16[1,2,8192,512]{3,1,0,2:T(2,128)(2,1)}) %all-gather.2.cloned.1.call-update) | async-done | bytes 16777232 | tf_op jit(solution)/shard_map/all_gather | solution.py:29
  166.0 32.7 %fusion.27 = (bf16[1,1,8192,512]{3,1,0,2:T(2,128)(2,1)}, bf16[1,1,8192,512]{3,1,0,2:T(2,128)(2,1)}) fusion(bf16[1,2,8192,512]{3,1,0,2:T(2,128)(2,1)} %all-gather.2.cloned.1.call-done), kind=kLoop, calls=%fused_computation.40 | loop fusion | bytes 33554432 | tf_op jit(solution)/shard_map/slice | solution.py:38
  198.7 33.4 %copy.46 = bf16[1,1,8192,512]{2,3,1,0:T(8,128)(2,1)} copy(bf16[1,1,8192,512]{3,1,0,2:T(2,128)(2,1)} %get-tuple-element.11) | data formatting | bytes 16777216
  232.1 33.3 %copy.45 = bf16[1,1,8192,512]{2,3,1,0:T(8,128)(2,1)} copy(bf16[1,1,8192,512]{3,1,0,2:T(2,128)(2,1)} %get-tuple-element.10) | data formatting | bytes 16777216
  265.4 16.0 %fusion = (f32[4,4,64]{2,1,0:T(4,128)S(1)}, f32[4,8192,64,4]{1,2,3,0:T(8,128)}) fusion(pred[64,8192]{1,0:T(8,128)(4,1)S(1)} %or_and_fusion, bf16[8192,4,128,1]{0,2,3,1:T(8,128)(2,1)} %bitcast.67, bf16[64,4,4,128]{3,2,1,0:T(4,128)(2,1)S(1)} %reshape_squeeze.13), kind=kOutput, calls=%fused_computation.5 | convolution fusion | flops 2172648448 | bytes 42733568 | tf_op jit(solution)/shard_map/qhgd,khd->hgqk/dot_general | solution.py:41
  281.4 15.2 %fusion.3 = f32[4,4,64]{2,1,0:T(4,128)S(1)} fusion(f32[4,8192,64,4]{1,2,3,0:T(8,128)} %get-tuple-element.13, f32[4,4,64]{2,1,0:T(4,128)S(1)} %broadcast_maximum_fusion, pred[64,8192]{1,0:T(8,128)(4,1)S(1)} %or_and_fusion), kind=kLoop, calls=%fused_computation.8 | loop fusion | flops 33553408 | bytes 34086912 | tf_op jit(solution)/shard_map/reduce_sum | solution.py:49
  296.6 15.9 %fusion.17 = bf16[64,4,4,128]{3,0,2,1:T(8,128)(2,1)S(1)} fusion(bf16[8192,4,128,1]{0,2,3,1:T(8,128)(2,1)} %bitcast.68, f32[4,8192,64,4]{1,2,3,0:T(8,128)} %get-tuple-element.13, f32[4,4,64]{2,1,0:T(4,128)S(1)} %broadcast_maximum_fusion, pred[64,8192]{1,0:T(8,128)(4,1)S(1)} %or_and_fusion, f32[64,4,4]{0,2,1:T(4,128)S(1)} %bitcast.71, ...), kind=kOutput, calls=%fused_computation.16 | convolution fusion | flops 2181431296 | bytes 42737728 | tf_op jit(solution)/shard_map/hgqk,khd->hgqd/dot_general | solution.py:50
  312.6 0.2 copy.32
  312.8 0.9 convert_element_type.19
  (11 shorter events, 0.1 us)
Async XLA Ops:
  7.2 158.8 %all-gather.2.cloned.1.call-start = ((), (), s32[]{:S(2)}) async-start(), calls=%async_computation.1 | async-start | bytes 16908288 | tf_op jit(solution)/shard_map/all_gather | solution.py:29
  12.7 27.6 %all-to-all-start = ((bf16[2,128,2,1,128]{4,2,0,3,1:T(2,128)(2,1)}), bf16[2,128,2,1,128]{4,2,0,3,1:T(2,128)(2,1)S(1)}, u32[]{:S(2)}, u32[]{:S(2)}) async-start(bf16[2,128,2,1,128]{4,2,0,3,1:T(2,128)(2,1)} %copy.35), calls=%async_computation | async-start | bytes 262144 | tf_op jit(solution)/shard_map/all_to_all | solution.py:69
Sparse Core Ops, SparseCore 0:
  12.0 153.9 all-gather.1
where the time goes:
time: 323 us; the launch traced here: 321 us
  waiting for transfers between devices  122 us (38%)
  local copies, waits for them, and re-layouts  116 us (36%)
  matrix products  31.9 us (10%)
  other arithmetic  19.4 us (6%)
  starting transfers between devices  16.6 us (5%)
  between operations  14.9 us (5%)
    all_gather x1, waiting for transfers between devices, body(): segment_piece = lax.all_gather(rotated_key_value, 'blk', axis=2, tiled=True)  117 us
    unnamed x4, local copies, waits for them, and re-layouts  69.1 us
    slice x1, local copies, waits for them, and re-layouts, body(): segment_piece[0, 0].reshape(row_indices, KEY_VALUE_HEADS, HEAD_DIMENSION)  32.7 us
    all_to_all x1, starting transfers between devices, body(): lax.all_to_all(outgoing, 'blk', split_axis=1, concat_axis=1, tiled=True)  16.5 us
    dot_general x1, matrix products, body(): jnp.einsum('qhgd,khd->hgqk', query_rows, key_rows, preferred_element_type...  16 us
    dot_general x1, matrix products, body(): jnp.einsum('hgqk,khd->hgqd', prob.astype(jnp.bfloat16), value_rows, prefe...  15.9 us
    reduce_sum x1, other arithmetic, body(): total = jnp.sum(prob, axis=-1)  15.2 us
    scatter x1, local copies, waits for them, and re-layouts, body(): held = jnp.zeros((2, prompt_blocks, group_repeats, HEAD_DIMENSION), jnp.b...  7.17 us
  transfers between devices with their start and end apart: 2, of which 2 were waited for; matrix products, arithmetic and copies ran while one was open for 6% of the time, Pallas kernels for 0%

commit v1 on v0

--- a/solution.py
+++ b/solution.py
@@ -26,7 +26,12 @@
     ).reshape(token_index)
     query_rows = query[0].reshape(token_index, KEY_VALUE_HEADS, query_groups, HEAD_DIMENSION)
     slot_seg = place % segment_list
-    segment_piece = lax.all_gather(rotated_key_value, "blk", axis=2, tiled=True)
+    segment_piece = jnp.concatenate(
+        jax.lax.all_to_all(
+            jnp.stack([rotated_key_value for _ in range(jax.lax.axis_size("blk"))]), "blk", 0, 0
+        ),
+        2,
+    )
     upper_limit = jnp.full((KEY_VALUE_HEADS, query_groups, token_index), -1e30, jnp.float32)
     held = jnp.zeros((2, prompt_blocks, group_repeats, HEAD_DIMENSION), jnp.bfloat16)
     row_indices = segment_piece.shape[2]

time: 323 us -> 503 us (1.56)
  waiting for transfers between devices: 122 us -> 354 us
  local copies, waits for them, and re-layouts: 116 us -> 56.8 us
  blocking collectives: 0 us -> 27.4 us
  between operations: 14.9 us -> 1.54 us
  starting transfers between devices: 16.6 us -> 7.89 us
    all_to_all x1, waiting for transfers between devices: 4.62 us -> 354 us  [body(): jax.lax.all_to_all(jnp.stack([rotated_key_value for _ in range(jax.lax.ax...]
    all_gather x1 -> x0, waiting for transfers between devices: 117 us -> none  [body(): segment_piece = lax.all_gather(rotated_key_value, 'blk', axis=2, tiled=True)]
    unnamed x4 -> x5, local copies, waits for them, and re-layouts: 69.1 us -> 0.68 us
    all_to_all x0 -> x1, blocking collectives: none -> 27.4 us  [body(): lax.all_to_all(outgoing, 'blk', split_axis=1, concat_axis=1, tiled=True)]
    slice x1 -> x2, local copies, waits for them, and re-layouts: 32.7 us -> 17.3 us  [body(): segment_piece[0, 0].reshape(row_indices, KEY_VALUE_HEADS, HEAD_DIMENSION)]
    slice x0 -> x1, local copies, waits for them, and re-layouts: none -> 11.3 us  [body(): segment_piece[0, 1].reshape(row_indices, KEY_VALUE_HEADS, HEAD_DIMENSION)]
    all_to_all x1, starting transfers between devices: 16.5 us -> 7.89 us  [body(): jax.lax.all_to_all(jnp.stack([rotated_key_value for _ in range(jax.lax.ax...]
    all_to_all x0 -> x1, local copies, waits for them, and re-layouts: none -> 8.2 us  [body(): jax.lax.all_to_all(jnp.stack([rotated_key_value for _ in range(jax.lax.ax...]
  transfers between devices with their start and end apart: 2 -> 1, of which waited for: 2 -> 1; matrix products, arithmetic and copies ran while one was open for 6% -> 2% of each run, Pallas kernels for 0% -> 0%
where the time goes in v1:
time: 503 us; the launch traced here: 498 us
  waiting for transfers between devices  354 us (70%)
  local copies, waits for them, and re-layouts  56.8 us (11%)
  matrix products  31.9 us (6%)
  blocking collectives  27.4 us (5%)
  other arithmetic  18 us (4%)
  starting transfers between devices  7.89 us (2%)
    all_to_all x1, waiting for transfers between devices, body(): jax.lax.all_to_all(jnp.stack([rotated_key_value for _ in range(jax.lax.ax...  354 us
    all_to_all x1, blocking collectives, body(): lax.all_to_all(outgoing, 'blk', split_axis=1, concat_axis=1, tiled=True)  27.4 us
    slice x2, local copies, waits for them, and re-layouts, body(): segment_piece[0, 0].reshape(row_indices, KEY_VALUE_HEADS, HEAD_DIMENSION)  17.3 us
    dot_general x1, matrix products, body(): jnp.einsum('qhgd,khd->hgqk', query_rows, key_rows, preferred_element_type...  16 us
    dot_general x1, matrix products, body(): jnp.einsum('hgqk,khd->hgqd', prob.astype(jnp.bfloat16), value_rows, prefe...  15.9 us
    reduce_sum x1, other arithmetic, body(): total = jnp.sum(prob, axis=-1)  15.2 us
    slice x1, local copies, waits for them, and re-layouts, body(): segment_piece[0, 1].reshape(row_indices, KEY_VALUE_HEADS, HEAD_DIMENSION)  11.3 us
  transfers between devices with their start and end apart: 1, of which 1 were waited for; matrix products, arithmetic and copies ran while one was open for 2% of the time, Pallas kernels for 0%

profile of v1, /device:TPU:1, one launch (start us, length us, event | category | flops | bytes accessed | tf_op | source)
XLA Modules:
  0.0 497.6 jit_solution(10395480810617388527)
XLA Ops:
  0.6 0.7 compare_select_fusion.1
  1.3 0.7 compare_and_fusion
  2.0 0.9 reshape.249
  2.9 0.6 gather_fusion.1
  3.5 0.1 fusion.22
  3.6 0.1 copy.37
  3.8 27.4 %all_to_all.10 = bf16[2,128,2,1,128]{4,2,0,3,1:T(2,128)(2,1)S(1)} all-to-all(bf16[2,128,2,1,128]{4,2,0,3,1:T(2,128)(2,1)S(1)} %copy.37), channel_id=1, replica_groups=mesh['req'=2,'blk'=128] {'blk'}, dimensions={1} | all-to-all | bytes 262144 | tf_op jit(solution)/shard_map/all_to_all | solution.py:74
  31.1 6.7 %stack.2 = bf16[128,1,2,64,512]{4,3,2,1,0:T(8,128)(2,1)} broadcast(bf16[2,64,512]{2,1,0:T(8,128)(2,1)} %bitcast.74), dimensions={2,3,4} | broadcast | bytes 16908288 | tf_op jit(solution)/shard_map/stack | solution.py:31
  37.8 0.0 copy-start
  37.8 0.0 copy-start.1
  37.9 7.9 %all-to-all-start = ((bf16[128,1,2,64,512]{4,3,2,1,0:T(8,128)(2,1)}), bf16[128,1,2,64,512]{4,3,2,1,0:T(8,128)(2,1)}, u32[]{:S(2)}, u32[]{:S(2)}) async-start(bf16[128,1,2,64,512]{4,3,2,1,0:T(8,128)(2,1)} %stack.2), calls=%async_computation | async-start | bytes 33554432 | tf_op jit(solution)/shard_map/all_to_all | solution.py:30
  45.8 0.0 copy-done
  45.8 1.9 gather_fusion
  47.8 0.1 iota_add_fusion
  47.9 0.1 add.100
  48.0 0.1 dynamic-slice_multiply_fusion
  48.0 0.1 iota_add_fusion.1
  48.1 0.1 add.96
  48.8 0.0 copy-done.1
  48.9 0.2 reshape_squeeze.13
  49.1 0.8 or_and_fusion
  49.9 0.1 copy.38
  50.0 0.1 copy.39
  50.1 0.1 broadcast.184
  50.2 7.2 %scatter_fusion = bf16[2,256,128]{2,0,1:T(2,128)(2,1)S(1)} fusion(bf16[2,256,128]{2,0,1:T(2,128)(2,1)S(1)} %broadcast.184, s32[256]{0:T(256)S(1)} %compare_select_fusion, bf16[256,2,128]{2,1,0:T(2,128)(2,1)S(1)} %copy.39), kind=kCustom, calls=%fused_computation.2 | custom fusion | bytes 394240 | tf_op jit(solution)/shard_map/scatter | solution.py:79
  57.4 0.3 fusion.23
  57.7 0.7 copy.40
  58.4 354.1 %all-to-all-done = bf16[128,1,2,64,512]{4,3,2,1,0:T(8,128)(2,1)} async-done(((bf16[128,1,2,64,512]{4,3,2,1,0:T(8,128)(2,1)}), bf16[128,1,2,64,512]{4,3,2,1,0:T(8,128)(2,1)}, u32[]{:S(2)}, u32[]{:S(2)}) %all-to-all-start) | async-done | bytes 16777248 | tf_op jit(solution)/shard_map/all_to_all | solution.py:30
  412.5 8.2 %copy.28 = bf16[128,1,2,64,512]{4,3,0,2,1:T(8,128)(2,1)S(1)} copy(bf16[128,1,2,64,512]{4,3,2,1,0:T(8,128)(2,1)} %all-to-all-done) | data formatting | bytes 33554432 | tf_op jit(solution)/shard_map/all_to_all | solution.py:30
  420.7 6.0 %fusion.27 = (bf16[1,1,8192,512]{3,2,1,0:T(8,128)(2,1)}, bf16[1,1,8192,512]{3,2,1,0:T(8,128)(2,1)}) fusion(bf16[1,2,8192,512]{3,2,1,0:T(8,128)(2,1)S(1)} %bitcast.71), kind=kLoop, calls=%fused_computation.40 | loop fusion | bytes 33554432 | tf_op jit(solution)/shard_map/slice | solution.py:43
  426.7 11.3 %copy.32 = bf16[1,1,8192,512]{2,3,1,0:T(8,128)(2,1)} copy(bf16[1,1,8192,512]{3,2,1,0:T(8,128)(2,1)} %get-tuple-element.11) | data formatting | bytes 16777216 | tf_op jit(solution)/shard_map/slice | solution.py:44
  438.0 11.3 %copy.29 = bf16[1,1,8192,512]{2,3,1,0:T(8,128)(2,1)} copy(bf16[1,1,8192,512]{3,2,1,0:T(8,128)(2,1)} %get-tuple-element.10) | data formatting | bytes 16777216 | tf_op jit(solution)/shard_map/slice | solution.py:43
  449.3 16.0 %fusion = (f32[4,4,64]{2,1,0:T(4,128)S(1)}, f32[4,8192,64,4]{1,2,3,0:T(8,128)}) fusion(pred[64,8192]{1,0:T(8,128)(4,1)S(1)} %or_and_fusion, bf16[8192,4,128,1]{0,2,3,1:T(8,128)(2,1)} %bitcast.72, bf16[64,4,4,128]{3,2,1,0:T(4,128)(2,1)S(1)} %reshape_squeeze.13), kind=kOutput, calls=%fused_computation.5 | convolution fusion | flops 2172648448 | bytes 42733568 | tf_op jit(solution)/shard_map/qhgd,khd->hgqk/dot_general | solution.py:46
  465.3 15.2 %fusion.3 = f32[4,4,64]{2,1,0:T(4,128)S(1)} fusion(f32[4,8192,64,4]{1,2,3,0:T(8,128)} %get-tuple-element.13, f32[4,4,64]{2,1,0:T(4,128)S(1)} %broadcast_maximum_fusion, pred[64,8192]{1,0:T(8,128)(4,1)S(1)} %or_and_fusion), kind=kLoop, calls=%fused_computation.8 | loop fusion | flops 33553408 | bytes 34086912 | tf_op jit(solution)/shard_map/reduce_sum | solution.py:54
  480.5 15.9 %fusion.17 = bf16[64,4,4,128]{3,0,2,1:T(8,128)(2,1)S(1)} fusion(bf16[8192,4,128,1]{0,2,3,1:T(8,128)(2,1)} %bitcast.73, f32[4,8192,64,4]{1,2,3,0:T(8,128)} %get-tuple-element.13, f32[4,4,64]{2,1,0:T(4,128)S(1)} %broadcast_maximum_fusion, pred[64,8192]{1,0:T(8,128)(4,1)S(1)} %or_and_fusion, f32[64,4,4]{0,2,1:T(4,128)S(1)} %bitcast.77, ...), kind=kOutput, calls=%fused_computation.16 | convolution fusion | flops 2181431296 | bytes 42737728 | tf_op jit(solution)/shard_map/hgqk,khd->hgqd/dot_general | solution.py:55
  496.5 0.2 copy.34
  496.7 0.9 convert_element_type.19
  (12 shorter events, 0.1 us)
Async XLA Ops:
  37.8 7.9 %copy-start = (s32[256]{0:T(256)S(1)}, s32[256]{0:T(256)}, u32[]{:S(2)}) copy-start(s32[256]{0:T(256)} %param.8) | copy-start | bytes 3076
  37.8 11.0 %copy-start.1 = (bf16[1,64,2048]{2,1,0:T(8,128)(2,1)S(1)}, bf16[1,64,2048]{2,1,0:T(8,128)(2,1)}, u32[]{:S(2)}) copy-start(bf16[1,64,2048]{2,1,0:T(8,128)(2,1)} %param.5) | copy-start | bytes 786436
  37.9 374.6 %all-to-all-start = ((bf16[128,1,2,64,512]{4,3,2,1,0:T(8,128)(2,1)}), bf16[128,1,2,64,512]{4,3,2,1,0:T(8,128)(2,1)}, u32[]{:S(2)}, u32[]{:S(2)}) async-start(bf16[128,1,2,64,512]{4,3,2,1,0:T(8,128)(2,1)} %stack.2), calls=%async_computation | async-start | bytes 33554432 | tf_op jit(solution)/shard_map/all_to_all | solution.py:30
